TPU v7x, 32 devices: a whole 2x2x4 slice. The times are simulated.
32 devices in a mesh: row: 16 (over z, y, core), col: 2 (over x).
Axes of the slice: x: 2, y: 2, z: 4, core: 2. Of those that a mesh axis runs over, the one named last changes fastest.
Arguments:
- pair: bfloat16 [384, 384, 128], P('row', 'col'), may hold values from -6 to 6
- gain: float32 [128], replicated, may hold values from 0.1 to 1.9
- projections: bfloat16 [5, 128, 128], replicated, may hold values from -0.5 to 0.5
- bias_weight: bfloat16 [128, 4], replicated, as said below
- valid_len: int32 [1], replicated, may hold values from 192 to 384
- out_cotangent: bfloat16 [384, 384, 128], P('row', 'col'), may hold values from -6 to 6
Outputs:
- attended: bfloat16 [384, 384, 128], P('row', 'col')
- pair_gradient: float32 [384, 384, 128], P('row', 'col')
- projection_grad: float32 [5, 128, 128], replicated
- bias_weight_grad: float32 [128, 4], replicated
- gain_gradient: float32 [128], replicated
Inputs may be any that keep to these rules, and one draw needn't show every extreme that they name: `bias_weight`: scale of the bias projection entries is free; rows are drawn independently.
All inputs are finite; a program needn't handle non-finite values.
Results may differ from a plain program's by a relative error of at most 0.0045.
The roundings to bfloat16 on the way count: a program that leaves them out, or rounds other values in their place, can miss the bound.
Values may be sent and summed in bfloat16 or wider, within the bound.
A program may use at most 64 MiB of HBM per device.

v0:
```python
import jax
import jax.numpy as jnp
from jax import lax
from jax.sharding import PartitionSpec as P

QB = 384
EPS = 1e-05


def dense(left, right):
    return jnp.einsum("abc,cd->abd", left, right, preferred_element_type=jnp.float32)


def outer_sum(left, right):
    return jnp.einsum("abc,abd->cd", left, right, preferred_element_type=jnp.float32)


def attend_forward(query, key, value, bias_blocks, keep):
    ncols, rows, heads, width = query.shape
    nblocks = bias_blocks.shape[0]
    scale = width ** (-0.5)

    def per_column(cols):
        qcol, kcol, vcol = cols

        def per_block(blk):
            qblk, bblk = blk
            scores = (
                jnp.einsum("qhd,khd->hqk", qblk, kcol, preferred_element_type=jnp.float32) * scale
                + bblk
            )
            scores = jnp.where(keep[None, None, :], scores, -1000000000.0)
            probs = jax.nn.softmax(scores, axis=-1)
            out = jnp.einsum(
                "hqk,khd->qhd", probs.astype(jnp.bfloat16), vcol, preferred_element_type=jnp.float32
            )
            return out.astype(jnp.bfloat16)

        return lax.map(
            per_block, (qcol.reshape(nblocks, rows // nblocks, heads, width), bias_blocks)
        ).reshape(rows, heads, width)

    return lax.map(per_column, (query, key, value))


def attend_backward(query, key, value, d_context, bias_blocks, keep):
    ncols, rows, heads, width = query.shape
    nblocks = bias_blocks.shape[0]
    qsize = rows // nblocks
    scale = width ** (-0.5)

    def per_column(total, cols):
        qcol, kcol, vcol, dcol = cols

        def per_block(carry, blk):
            dk_acc, dv_acc = carry
            qblk, dblk, bblk = blk
            scores = (
                jnp.einsum("qhd,khd->hqk", qblk, kcol, preferred_element_type=jnp.float32) * scale
                + bblk
            )
            scores = jnp.where(keep[None, None, :], scores, -1000000000.0)
            probs = jax.nn.softmax(scores, axis=-1)
            weights_b = probs.astype(jnp.bfloat16)
            d_probs = jnp.einsum("qhd,khd->hqk", dblk, vcol, preferred_element_type=jnp.float32)
            d_scores = probs * (d_probs - jnp.sum(probs * d_probs, axis=-1, keepdims=True))
            dsb = d_scores.astype(jnp.bfloat16)
            dq = (
                jnp.einsum("hqk,khd->qhd", dsb, kcol, preferred_element_type=jnp.float32) * scale
            ).astype(jnp.bfloat16)
            dk_acc = (
                dk_acc
                + jnp.einsum("hqk,qhd->khd", dsb, qblk, preferred_element_type=jnp.float32) * scale
            )
            dv_acc = dv_acc + jnp.einsum(
                "hqk,qhd->khd", weights_b, dblk, preferred_element_type=jnp.float32
            )
            return ((dk_acc, dv_acc), (dq, d_scores))

        zeros = jnp.zeros((rows, heads, width), jnp.float32)
        (dk, dv), (dq, dscores) = lax.scan(
            per_block,
            (zeros, zeros),
            (
                qcol.reshape(nblocks, qsize, heads, width),
                dcol.reshape(nblocks, qsize, heads, width),
                bias_blocks,
            ),
        )
        return (
            total + dscores,
            (dq.reshape(rows, heads, width), dk.astype(jnp.bfloat16), dv.astype(jnp.bfloat16)),
        )

    start = jnp.zeros(bias_blocks.shape, jnp.float32)
    total, (dq, dk, dv) = lax.scan(per_column, start, (query, key, value, d_context))
    return (dq, dk, dv, total)


def arrange_bias(gathered, n_row, n_col, rows):
    heads, tile_rows, tile_cols = (gathered.shape[1], gathered.shape[2], gathered.shape[3])
    grid = gathered.reshape(n_row, n_col, heads, tile_rows, tile_cols)
    bias_t = jnp.transpose(grid, (2, 1, 4, 0, 3)).reshape(heads, rows, rows)
    return bias_t.reshape(heads, rows // QB, QB, rows).transpose(1, 0, 2, 3)


def shards(pair, gain, projections, bias_weight, valid_len, out_cotangent):
    n_row = lax.axis_size("row")
    n_col = lax.axis_size("col")
    tile_rows, tile_cols, channels = pair.shape
    rows = tile_rows * n_row
    heads = bias_weight.shape[1]
    width = channels // heads
    ncols = tile_cols // n_row
    pair_float = pair.astype(jnp.float32)
    average_value = jnp.mean(pair_float, axis=-1, keepdims=True)
    var = jnp.mean((pair_float - average_value) ** 2, axis=-1, keepdims=True)
    inverse_deviation = lax.rsqrt(var + EPS)
    centered_scaled = (pair_float - average_value) * inverse_deviation
    normalized_pair = (centered_scaled * gain).astype(jnp.bfloat16)
    bias_tile = jnp.einsum(
        "abc,ch->hab", normalized_pair, bias_weight, preferred_element_type=jnp.float32
    )
    gathered = lax.all_gather(bias_tile[None], ("row", "col"), axis=0, tiled=True)
    bias_blocks = arrange_bias(gathered, n_row, n_col, rows)
    keep = jnp.arange(rows, dtype=jnp.int32) < valid_len[0]

    def split(tensor):
        return jnp.moveaxis(tensor, 1, 0).reshape(ncols, rows, heads, width)

    def join(tensor):
        return jnp.moveaxis(tensor.reshape(ncols, rows, channels), 0, 1)

    normed_cols, cot_cols = (
        lax.all_to_all(normalized_pair, "row", split_axis=1, concat_axis=0, tiled=True),
        lax.all_to_all(out_cotangent, "row", split_axis=1, concat_axis=0, tiled=True),
    )
    query = dense(normed_cols, projections[0]).astype(jnp.bfloat16)
    key = dense(normed_cols, projections[1]).astype(jnp.bfloat16)
    value = dense(normed_cols, projections[2]).astype(jnp.bfloat16)
    gate = jax.nn.sigmoid(dense(normed_cols, projections[3]))
    qcols, kcols, vcols = (split(query), split(key), split(value))
    context = join(attend_forward(qcols, kcols, vcols, bias_blocks, keep))
    gated = (gate * context.astype(jnp.float32)).astype(jnp.bfloat16)
    attended_cols = dense(gated, projections[4]).astype(jnp.bfloat16)
    attended = lax.all_to_all(attended_cols, "row", split_axis=0, concat_axis=1, tiled=True)
    d_gated = dense(cot_cols, projections[4].T)
    d_context_cols = (d_gated * gate).astype(jnp.bfloat16)
    d_gate_pre = (d_gated * context.astype(jnp.float32) * gate * (1.0 - gate)).astype(jnp.bfloat16)
    dq, dk, dv, total = attend_backward(
        qcols, kcols, vcols, split(d_context_cols), bias_blocks, keep
    )
    dq, dk, dv = (join(dq), join(dk), join(dv))
    grid = total.transpose(1, 0, 2, 3).reshape(heads, n_col, tile_cols, n_row, tile_rows)
    grid = jnp.transpose(grid, (3, 1, 0, 4, 2))
    flat = grid.reshape(n_row * n_col, heads, tile_rows, tile_cols)
    d_bias = lax.psum_scatter(flat, ("row", "col"), scatter_dimension=0, tiled=True)[0].astype(
        jnp.bfloat16
    )
    bias_term = jnp.einsum("hab,ch->abc", d_bias, bias_weight, preferred_element_type=jnp.float32)
    bias_weight_part = jnp.einsum(
        "abc,hab->ch", normalized_pair, d_bias, preferred_element_type=jnp.float32
    )
    d_cols = dense(dq, projections[0].T) + dense(dk, projections[1].T) + dense(dv, projections[2].T)
    d_cols = d_cols + dense(d_gate_pre, projections[3].T)
    parts = jnp.stack(
        [
            outer_sum(normed_cols, dq),
            outer_sum(normed_cols, dk),
            outer_sum(normed_cols, dv),
            outer_sum(normed_cols, d_gate_pre),
            outer_sum(gated, cot_cols),
        ]
    )
    normalized_gradient = (
        lax.all_to_all(d_cols, "row", split_axis=0, concat_axis=1, tiled=True) + bias_term
    )
    gain_partial_sum = jnp.sum(normalized_gradient * centered_scaled, axis=(0, 1))
    projection_grad, bias_weight_grad, gain_gradient = lax.psum(
        (parts, bias_weight_part, gain_partial_sum), ("row", "col")
    )
    scaled_output = normalized_gradient * gain
    pair_gradient = inverse_deviation * (
        scaled_output
        - jnp.mean(scaled_output, axis=-1, keepdims=True)
        - centered_scaled * jnp.mean(scaled_output * centered_scaled, axis=-1, keepdims=True)
    )
    return (attended, pair_gradient, projection_grad, bias_weight_grad, gain_gradient)


def solution(mesh):
    placed = (P("row", "col", None), P(), P(), P(), P(), P("row", "col", None))
    return jax.shard_map(
        shards,
        mesh=mesh,
        in_specs=placed,
        out_specs=(P("row", "col", None), P("row", "col", None), P(), P(), P()),
        check_vma=False,
    )
```

profile of v0, /device:TPU:8, one launch (start us, length us, event | category | flops | bytes accessed | tf_op | source)
XLA Modules:
  0.0 754.6 jit_solution(17553295921628759125)
XLA Ops:
  14.7 6.3 all-to-all-start
  24.3 25.6 %all-to-all-done = bf16[24,192,128]{2,0,1:T(8,128)(2,1)S(1)} async-done(((bf16[24,192,128]{2,0,1:T(8,128)(2,1)}), bf16[24,192,128]{2,0,1:T(8,128)(2,1)S(1)}, u32[]{:S(2)}, u32[]{:S(2)}) %all-to-all-start) | async-done | bytes 1179680 | tf_op jit(solution)/shard_map/all_to_all | solution.py:135
  49.9 5.8 all-to-all-start.2
  56.0 38.6 %all-to-all-done.2 = bf16[24,192,128]{2,0,1:T(8,128)(2,1)S(1)} async-done(((bf16[24,192,128]{2,0,1:T(8,128)(2,1)}), bf16[24,192,128]{2,0,1:T(8,128)(2,1)S(1)}, u32[]{:S(2)}, u32[]{:S(2)}) %all-to-all-start.2) | async-done | bytes 1179680 | tf_op jit(solution)/shard_map/all_to_all | solution.py:136
  102.0 6.0 copy.150
  113.1 113.0 %while.28 = (s32[]{:T(128)}, bf16[12,384,4,32]{1,3,2,0:T(8,128)(2,1)}, bf16[12,384,4,32]{1,3,2,0:T(8,128)(2,1)}, bf16[12,384,4,32]{1,3,2,0:T(8,128)(2,1)}, bf16[...) while((s32[]{:T(128)}, ...), condition=%wide.region_5.6_spmd.clone, body=%wide.region_2.5_spmd.clone.sunk | while | flops 119786112 | bytes 12402905 | solution.py:43
  226.1 4.9 fusion.92
  234.2 6.4 all-to-all-start.1
  244.1 230.7 %while.29 = (s32[]{:T(128)}, f32[1,4,384,384]{2,3,1,0:T(8,128)}, bf16[12,384,4,32]{1,3,2,0:T(8,128)(2,1)}, bf16[12,384,4,32]{1,3,2,0:T(8,128)(2,1)}, bf16[12,384...) while((s32[]{:T(128)}, f32[1,4,384,384]{2,3,1,0:T(8,128)}, ...), condition=%wide.region_10.11_spmd.clone, body=%wide.region_6.10_spmd.clone.sunk | while | flops 240305280 | bytes 59063672 | solution.py:96
  273.6 4.5 bitcast_add_fusion.4
  292.9 4.5 bitcast_add_fusion.4
  312.2 4.5 bitcast_add_fusion.4
  331.5 4.5 bitcast_add_fusion.4
  350.7 4.5 bitcast_add_fusion.4
  370.0 4.5 bitcast_add_fusion.4
  389.3 4.5 bitcast_add_fusion.4
  408.6 4.5 bitcast_add_fusion.4
  427.9 4.5 bitcast_add_fusion.4
  447.2 4.5 bitcast_add_fusion.4
  488.9 6.2 all-to-all-start.3
  513.3 99.0 %reduce-scatter.2.cloned.1.call-done = f32[1,4,24,192]{3,2,1,0:T(8,128)} async-done(((f32[32,4,24,192]{3,2,1,0:T(8,128)}), f32[1,4,24,192]{3,2,1,0:T(8,128)}) %reduce-scatter.2.cloned.1.call-update) | async-done | bytes 73744 | tf_op jit(solution)/shard_map/reduce_scatter | solution.py:157
  620.3 4.8 fusion.84
  625.1 39.1 %all-reduce = (f32[128,4]{0,1:T(4,128)}, f32[128]{0:T(128)}) all-reduce(f32[128,4]{0,1:T(4,128)S(1)} %convolution_bitcast_fusion.3, f32[128]{0:T(128)S(1)} %get-tuple-element.237), channel_id=1, replica_groups=mesh['row'=16,'col'=2] {'row','col'}, use_global_device_ids=true, to_apply=%region_15.16 | all-reduce | flops 640 | bytes 5120 | tf_op jit(solution)/shard_map/psum | solution.py:179
  664.1 82.2 %all-reduce.3.cloned.1.call-done = f32[5,128,128]{2,1,0:T(8,128)} async-done(((f32[5,128,128]{2,1,0:T(8,128)}), f32[5,128,128]{2,1,0:T(8,128)}) %all-reduce.3.cloned.1.call-update) | async-done | bytes 327696 | tf_op jit(solution)/shard_map/psum | solution.py:179
  (339 shorter events, 370.2 us)
Async XLA Ops:
  7.2 13.9 %copy-start = (bf16[128,4]{0,1:T(4,128)(2,1)S(1)}, bf16[128,4]{0,1:T(4,128)(2,1)}, u32[]{:S(2)}) copy-start(bf16[128,4]{0,1:T(4,128)(2,1)} %param.13) | copy-start | bytes 3076
  7.2 4.3 copy-start.29
  12.9 8.1 %copy-start.5 = (bf16[24,192,128]{2,1,0:T(8,128)(2,1)}, bf16[24,192,128]{2,1,0:T(8,128)(2,1)S(1)}, u32[]{:S(2)}) copy-start(bf16[24,192,128]{2,1,0:T(8,128)(2,1)S(1)} %fusion.81) | copy-start | bytes 3538948
  14.7 35.2 %all-to-all-start = ((bf16[24,192,128]{2,0,1:T(8,128)(2,1)}), bf16[24,192,128]{2,0,1:T(8,128)(2,1)S(1)}, u32[]{:S(2)}, u32[]{:S(2)}) async-start(bf16[24,192,128]{2,0,1:T(8,128)(2,1)} %copy.143), calls=%async_computation | async-start | bytes 2359296 | tf_op jit(solution)/shard_map/all_to_all | solution.py:135
  21.0 81.0 %all-gather.3.cloned.1.call-start = ((), (), s32[]{:S(2)}) async-start(), calls=%async_computation.7 | async-start | bytes 3244032 | tf_op jit(solution)/shard_map/all_gather | solution.py:124
  49.9 44.7 %all-to-all-start.2 = ((bf16[24,192,128]{2,0,1:T(8,128)(2,1)}), bf16[24,192,128]{2,0,1:T(8,128)(2,1)S(1)}, u32[]{:S(2)}, u32[]{:S(2)}) async-start(bf16[24,192,128]{2,0,1:T(8,128)(2,1)} %copy.155), calls=%async_computation.2 | async-start | bytes 2359296 | tf_op jit(solution)/shard_map/all_to_all | solution.py:136
  94.8 5.3 copy-start.9
  234.2 254.7 %all-to-all-start.1 = ((bf16[384,12,128]{2,1,0:T(8,128)(2,1)}), bf16[384,12,128]{2,1,0:T(8,128)(2,1)}, u32[]{:S(2)}, u32[]{:S(2)}) async-start(bf16[384,12,128]{2,1,0:T(8,128)(2,1)} %copy.152), calls=%async_computation.1 | async-start | bytes 3145728 | tf_op jit(solution)/shard_map/all_to_all | solution.py:146
  258.8 3.8 copy-start.2
  278.1 3.8 copy-start.2
  297.4 3.8 copy-start.2
  336.0 3.8 copy-start.2
  355.2 3.8 copy-start.2
  374.5 3.8 copy-start.2
  393.8 3.8 copy-start.2
  413.1 3.8 copy-start.2
  432.4 3.8 copy-start.2
  476.5 5.0 copy-start.13
  478.6 4.1 copy-start.11
  488.9 6.2 copy-start.4
  488.9 124.7 %all-to-all-start.3 = ((f32[384,12,128]{2,1,0:T(8,128)}), f32[384,12,128]{2,1,0:T(8,128)}, u32[]{:S(2)}, u32[]{:S(2)}) async-start(f32[384,12,128]{2,1,0:T(8,128)} %copy.165), calls=%async_computation.3 | async-start | bytes 6291456 | tf_op jit(solution)/shard_map/all_to_all | solution.py:176
  495.0 117.3 %reduce-scatter.2.cloned.1.call-start = ((), (), s32[]{:S(2)}) async-start(), calls=%async_computation.5 | async-start | bytes 3244032 | tf_op jit(solution)/shard_map/reduce_scatter | solution.py:157
  502.6 243.7 %all-reduce.3.cloned.1.call-start = ((), (), s32[]{:S(2)}) async-start(), calls=%async_computation.6 | async-start | bytes 655360 | tf_op jit(solution)/shard_map/psum | solution.py:179
  512.0 101.2 %copy-start.6 = (bf16[24,192,128]{2,1,0:T(8,128)(2,1)S(1)}, bf16[24,192,128]{2,1,0:T(8,128)(2,1)}, u32[]{:S(2)}) copy-start(bf16[24,192,128]{2,1,0:T(8,128)(2,1)} %copy-done.5) | copy-start | bytes 3538948
  (58 other events, 94.1 us)
Sparse Core Ops, SparseCore 0:
  25.3 71.1 all-gather.2
  502.7 109.5 reduce-scatter.1
  618.2 128.0 all-reduce.2
where the time goes:
time: 758 us; the launch traced here: 755 us
  matrix products  275 us (36%)
  waiting for transfers between devices  245 us (32%)
  other arithmetic  84.5 us (11%)
  local copies, waits for them, and re-layouts  71.3 us (9%)
  blocking collectives  39.1 us (5%)
  starting transfers between devices  25 us (3%)
  between operations  14.1 us (2%)
    reduce_scatter x1, waiting for transfers between devices, shards(): lax.psum_scatter(flat, ('row', 'col'), scatter_dimension=0, tiled=True)[0]  99 us
    psum x1, waiting for transfers between devices, shards(): lax.psum((parts, bias_weight_part, gain_partial_sum), ('row', 'col'))  82.2 us
    sub x24, matrix products, per_block(): probs = jax.nn.softmax(scores, axis=-1)  58.6 us
    add x12, other arithmetic, per_column(): total + dscores  53.3 us
    dot_general x12, matrix products, per_block(): jnp.einsum('hqk,qhd->khd', weights_b, dblk, preferred_element_type=jnp.fl...  45.7 us
    dot_general x12, matrix products, per_block(): jnp.einsum('hqk,khd->qhd', probs.astype(jnp.bfloat16), vcol, preferred_el...  44 us
    psum x1, blocking collectives, shards(): lax.psum((parts, bias_weight_part, gain_partial_sum), ('row', 'col'))  39.1 us
    all_to_all x1, waiting for transfers between devices, shards(): lax.all_to_all(out_cotangent, 'row', split_axis=1, concat_axis=0, tiled=T...  38.6 us
  transfers between devices with their start and end apart: 7, of which 4 were waited for; matrix products, arithmetic and copies ran while one was open for 35% of the time, Pallas kernels for 0%

commit v1 on v0

--- a/solution.py
+++ b/solution.py
@@ -177,7 +177,7 @@
     )
     gain_partial_sum = jnp.sum(normalized_gradient * centered_scaled, axis=(0, 1))
     projection_grad, bias_weight_grad, gain_gradient = lax.psum(
-        (parts, bias_weight_part, gain_partial_sum), ("row", "col")
+        lax.psum((parts, bias_weight_part, gain_partial_sum), "row"), "col"
     )
     scaled_output = normalized_gradient * gain
     pair_gradient = inverse_deviation * (

time: 758 us -> 799 us (1.054); the launches traced: 755 us -> 786 us
  waiting for transfers between devices: 245 us -> 285 us
  blocking collectives: 39.1 us -> 28.8 us
    psum x1 -> x2, waiting for transfers between devices: 82.2 us -> 118 us  [the longest x1 118 us: shards(): lax.psum((parts, bias_weight_part, gain_partial_sum), 'row')]
    psum x1 -> x2, blocking collectives: 39.1 us -> 28.8 us  [the longest x1 23.2 us: shards(): lax.psum((parts, bias_weight_part, gain_partial_sum), 'row')]
  transfers between devices with their start and end apart: 7 -> 8, of which waited for: 4 -> 4; matrix products, arithmetic and copies ran while one was open for 35% -> 34% of each run, Pallas kernels for 0% -> 0%
where the time goes in v1:
time: 799 us; the launch traced here: 786 us
  waiting for transfers between devices  285 us (36%)
  matrix products  276 us (35%)
  other arithmetic  86 us (11%)
  local copies, waits for them, and re-layouts  69.3 us (9%)
  blocking collectives  28.8 us (4%)
  starting transfers between devices  24.9 us (3%)
  between operations  14.1 us (2%)
    psum x1, waiting for transfers between devices, shards(): lax.psum((parts, bias_weight_part, gain_partial_sum), 'row')  118 us
    reduce_scatter x1, waiting for transfers between devices, shards(): lax.psum_scatter(flat, ('row', 'col'), scatter_dimension=0, tiled=True)[0]  103 us
    sub x24, matrix products, per_block(): probs = jax.nn.softmax(scores, axis=-1)  58.6 us
    add x12, other arithmetic, per_column(): total + dscores  53 us
    dot_general x12, matrix products, per_block(): jnp.einsum('hqk,qhd->khd', weights_b, dblk, preferred_element_type=jnp.fl...  45.7 us
    dot_general x12, matrix products, per_block(): jnp.einsum('hqk,khd->qhd', probs.astype(jnp.bfloat16), vcol, preferred_el...  44 us
    all_to_all x1, waiting for transfers between devices, shards(): lax.all_to_all(out_cotangent, 'row', split_axis=1, concat_axis=0, tiled=T...  38.6 us
    dot_general x12, matrix products, per_block(): jnp.einsum('qhd,khd->hqk', qblk, kcol, preferred_element_type=jnp.float32)  36.6 us
  transfers between devices with their start and end apart: 8, of which 4 were waited for; matrix products, arithmetic and copies ran while one was open for 34% of the time, Pallas kernels for 0%

profile of v1, /device:TPU:8, one launch (start us, length us, event | category | flops | bytes accessed | tf_op | source)
XLA Modules:
  0.0 785.5 jit_solution(8486345230077181120)
XLA Ops:
  14.1 6.3 all-to-all-start
  23.7 25.6 %all-to-all-done = bf16[24,192,128]{2,0,1:T(8,128)(2,1)S(1)} async-done(((bf16[24,192,128]{2,0,1:T(8,128)(2,1)}), bf16[24,192,128]{2,0,1:T(8,128)(2,1)S(1)}, u32[]{:S(2)}, u32[]{:S(2)}) %all-to-all-start) | async-done | bytes 1179680 | tf_op jit(solution)/shard_map/all_to_all | solution.py:135
  49.3 5.8 all-to-all-start.2
  55.4 38.6 %all-to-all-done.2 = bf16[24,192,128]{2,0,1:T(8,128)(2,1)S(1)} async-done(((bf16[24,192,128]{2,0,1:T(8,128)(2,1)}), bf16[24,192,128]{2,0,1:T(8,128)(2,1)S(1)}, u32[]{:S(2)}, u32[]{:S(2)}) %all-to-all-start.2) | async-done | bytes 1179680 | tf_op jit(solution)/shard_map/all_to_all | solution.py:136
  101.5 6.0 copy.150
  112.5 113.1 %while.28 = (s32[]{:T(128)}, bf16[12,384,4,32]{1,3,2,0:T(8,128)(2,1)}, bf16[12,384,4,32]{1,3,2,0:T(8,128)(2,1)}, bf16[12,384,4,32]{1,3,2,0:T(8,128)(2,1)}, bf16[...) while((s32[]{:T(128)}, ...), condition=%wide.region_5.6_spmd.clone, body=%wide.region_2.5_spmd.clone.sunk | while | flops 119786112 | bytes 12402905 | solution.py:43
  225.6 4.9 fusion.92
  233.8 6.4 all-to-all-start.1
  243.6 230.4 %while.29 = (s32[]{:T(128)}, f32[1,4,384,384]{2,3,1,0:T(8,128)}, bf16[12,384,4,32]{1,3,2,0:T(8,128)(2,1)}, bf16[12,384,4,32]{1,3,2,0:T(8,128)(2,1)}, bf16[12,384...) while((s32[]{:T(128)}, f32[1,4,384,384]{2,3,1,0:T(8,128)}, ...), condition=%wide.region_10.11_spmd.clone, body=%wide.region_6.10_spmd.clone.sunk | while | flops 240305280 | bytes 59063672 | solution.py:96
  273.2 4.5 bitcast_add_fusion.4
  292.4 4.5 bitcast_add_fusion.4
  311.7 4.5 bitcast_add_fusion.4
  330.9 4.5 bitcast_add_fusion.4
  350.2 4.5 bitcast_add_fusion.4
  369.5 4.5 bitcast_add_fusion.4
  388.7 4.5 bitcast_add_fusion.4
  446.5 4.5 bitcast_add_fusion.4
  489.6 6.0 all-to-all-start.3
  508.0 117.6 %all-reduce.5.cloned.1.call-done = f32[5,128,128]{2,1,0:T(8,128)} async-done(((f32[5,128,128]{2,1,0:T(8,128)}), f32[5,128,128]{2,1,0:T(8,128)}) %all-reduce.5.cloned.1.call-update) | async-done | bytes 327696 | tf_op jit(solution)/shard_map/psum | solution.py:180
  628.7 103.5 %reduce-scatter.2.cloned.1.call-done = f32[1,4,24,192]{3,2,1,0:T(8,128)} async-done(((f32[32,4,24,192]{3,2,1,0:T(8,128)}), f32[1,4,24,192]{3,2,1,0:T(8,128)}) %reduce-scatter.2.cloned.1.call-update) | async-done | bytes 73744 | tf_op jit(solution)/shard_map/reduce_scatter | solution.py:157
  736.2 5.6 fusion.85
  741.8 23.2 %all-reduce = (f32[128,4]{0,1:T(4,128)S(1)}, f32[128]{0:T(128)}) all-reduce(f32[128,4]{0,1:T(4,128)S(1)} %convolution_bitcast_fusion.3, f32[128]{0:T(128)} %get-tuple-element.237), channel_id=1, replica_groups=mesh['row'=16,'col'=2] {'row'}, use_global_device_ids=true, to_apply=%region_16.17 | all-reduce | flops 640 | bytes 5120 | tf_op jit(solution)/shard_map/psum | solution.py:180
  765.1 5.6 all-reduce.1
  771.4 5.9 fusion.84
  (335 shorter events, 374.1 us)
Async XLA Ops:
  7.2 13.3 %copy-start = (bf16[128,4]{0,1:T(4,128)(2,1)S(1)}, bf16[128,4]{0,1:T(4,128)(2,1)}, u32[]{:S(2)}) copy-start(bf16[128,4]{0,1:T(4,128)(2,1)} %param.13) | copy-start | bytes 3076
  12.4 8.1 %copy-start.5 = (bf16[24,192,128]{2,1,0:T(8,128)(2,1)}, bf16[24,192,128]{2,1,0:T(8,128)(2,1)S(1)}, u32[]{:S(2)}) copy-start(bf16[24,192,128]{2,1,0:T(8,128)(2,1)S(1)} %fusion.81) | copy-start | bytes 3538948
  14.1 35.2 %all-to-all-start = ((bf16[24,192,128]{2,0,1:T(8,128)(2,1)}), bf16[24,192,128]{2,0,1:T(8,128)(2,1)S(1)}, u32[]{:S(2)}, u32[]{:S(2)}) async-start(bf16[24,192,128]{2,0,1:T(8,128)(2,1)} %copy.143), calls=%async_computation | async-start | bytes 2359296 | tf_op jit(solution)/shard_map/all_to_all | solution.py:135
  20.4 81.1 %all-gather.3.cloned.1.call-start = ((), (), s32[]{:S(2)}) async-start(), calls=%async_computation.8 | async-start | bytes 3244032 | tf_op jit(solution)/shard_map/all_gather | solution.py:124
  49.3 44.7 %all-to-all-start.2 = ((bf16[24,192,128]{2,0,1:T(8,128)(2,1)}), bf16[24,192,128]{2,0,1:T(8,128)(2,1)S(1)}, u32[]{:S(2)}, u32[]{:S(2)}) async-start(bf16[24,192,128]{2,0,1:T(8,128)(2,1)} %copy.155), calls=%async_computation.2 | async-start | bytes 2359296 | tf_op jit(solution)/shard_map/all_to_all | solution.py:136
  94.3 5.4 copy-start.9
  233.8 255.9 %all-to-all-start.1 = ((bf16[384,12,128]{2,1,0:T(8,128)(2,1)}), bf16[384,12,128]{2,1,0:T(8,128)(2,1)}, u32[]{:S(2)}, u32[]{:S(2)}) async-start(bf16[384,12,128]{2,1,0:T(8,128)(2,1)} %copy.152), calls=%async_computation.1 | async-start | bytes 3145728 | tf_op jit(solution)/shard_map/all_to_all | solution.py:146
  258.4 3.8 copy-start.2
  277.6 3.8 copy-start.2
  296.9 3.8 copy-start.2
  316.2 3.8 copy-start.2
  335.4 3.8 copy-start.2
  354.7 3.8 copy-start.2
  374.0 3.8 copy-start.2
  393.2 3.8 copy-start.2
  412.5 3.8 copy-start.2
  431.8 3.8 copy-start.2
  451.0 3.8 copy-start.2
  470.3 3.8 copy-start.2
  489.6 243.8 %all-to-all-start.3 = ((f32[384,12,128]{2,1,0:T(8,128)}), f32[384,12,128]{2,1,0:T(8,128)}, u32[]{:S(2)}, u32[]{:S(2)}) async-start(f32[384,12,128]{2,1,0:T(8,128)} %copy.165), calls=%async_computation.3 | async-start | bytes 6291456 | tf_op jit(solution)/shard_map/all_to_all | solution.py:176
  495.6 130.0 %all-reduce.5.cloned.1.call-start = ((), (), s32[]{:S(2)}) async-start(), calls=%async_computation.6 | async-start | bytes 655360 | tf_op jit(solution)/shard_map/psum | solution.py:180
  499.7 232.4 %reduce-scatter.2.cloned.1.call-start = ((), (), s32[]{:S(2)}) async-start(), calls=%async_computation.5 | async-start | bytes 3244032 | tf_op jit(solution)/shard_map/reduce_scatter | solution.py:157
  507.7 269.6 %all-reduce.7.cloned.1.call-start = ((), (), s32[]{:S(2)}) async-start(), calls=%async_computation.7 | async-start | bytes 655360 | tf_op jit(solution)/shard_map/psum | solution.py:179
  627.4 105.7 %copy-start.6 = (bf16[24,192,128]{2,1,0:T(8,128)(2,1)S(1)}, bf16[24,192,128]{2,1,0:T(8,128)(2,1)}, u32[]{:S(2)}) copy-start(bf16[24,192,128]{2,1,0:T(8,128)(2,1)} %copy-done.5) | copy-start | bytes 3538948
  (55 other events, 88.6 us)
Sparse Core Ops, SparseCore 0:
  24.7 71.1 all-gather.2
  500.4 125.2 all-reduce.4
  631.1 101.0 reduce-scatter.1
  734.3 23.5 all-reduce.6
